TPU v7x, 32 devices: a whole 2x2x4 slice. The times are simulated.
32 devices in a mesh: dp: 8 (over z, y), ctx: 4 (over x, core).
Axes of the slice: x: 2, y: 2, z: 4, core: 2. Of those that a mesh axis runs over, the one named last changes fastest.
Arguments:
- tokens: bfloat16 [8, 1024, 1024], P('dp', 'ctx'), may hold values from -6 to 6
- doc_ids: int32 [8, 1024], P('dp', 'ctx'), may hold values from 0 to 7, never falling along the last dimension, each value on 1 to 512 neighbouring positions
- w_query: bfloat16 [1024, 1024], P(('dp', 'ctx')), may hold values from -0.1875 to 0.1875
- key_weight: bfloat16 [1024, 512], P(('dp', 'ctx')), may hold values from -0.1875 to 0.1875
- value_weight: bfloat16 [1024, 512], P(('dp', 'ctx')), may hold values from -0.1875 to 0.1875
- w_output: bfloat16 [1024, 1024], P(None, ('dp', 'ctx')), may hold values from -1.5 to 1.5
- w_gate: bfloat16 [1024, 4608], P(('dp', 'ctx')), may hold values from -0.1875 to 0.1875
- w_up: bfloat16 [1024, 4608], P(('dp', 'ctx')), may hold values from -0.1875 to 0.1875
- w_down: bfloat16 [4608, 1024], P(None, ('dp', 'ctx')), may hold values from -0.09375 to 0.09375
- norm_gains: bfloat16 [2, 1024], P(None, ('dp', 'ctx')), may hold values from 0.5 to 1.5
- head_norm_gains: bfloat16 [2, 64], replicated, may hold values from 0.5 to 1.5
- out_grad: bfloat16 [8, 1024, 1024], P('dp', 'ctx'), may hold values from -6 to 6
Outputs:
- layer_out: bfloat16 [8, 1024, 1024], P('dp', 'ctx')
- input_grad: bfloat16 [8, 1024, 1024], P('dp', 'ctx')
- grad_query: bfloat16 [1024, 1024], P(('dp', 'ctx'))
- grad_key: bfloat16 [1024, 512], P(('dp', 'ctx'))
- grad_value: bfloat16 [1024, 512], P(('dp', 'ctx'))
- grad_output: bfloat16 [1024, 1024], P(None, ('dp', 'ctx'))
- grad_gate: bfloat16 [1024, 4608], P(('dp', 'ctx'))
- grad_up: bfloat16 [1024, 4608], P(('dp', 'ctx'))
- grad_down: bfloat16 [4608, 1024], P(None, ('dp', 'ctx'))
- grad_norms: bfloat16 [2, 1024], P(None, ('dp', 'ctx'))
- grad_heads: bfloat16 [2, 64], replicated
Inputs may be any that keep to these rules, and one draw needn't show every extreme that they name: `doc_ids`: along each sequence the numbers never fall; each document spans 1 to 512 tokens.
All inputs are finite; a program needn't handle non-finite values.
Results may differ from a plain program's by a relative error of at most 0.015.
Values may be sent and summed in bfloat16 or wider, within the bound.
No kernel may reach another device: no remote copies, remote signals or barrier semaphores. Data moves between devices by JAX's collectives and lax.ppermute only.
A program may use at most 320 MiB of HBM per device.

v0:
```python
import math

import jax
import jax.numpy as jnp
from jax import lax
from jax.sharding import PartitionSpec as P

EPS = 1e-05
THETA = 1000000.0


def rms_scale(values, gain_row):
    return values * lax.rsqrt(jnp.mean(values * values, -1, keepdims=True) + EPS) * gain_row


def rope_tables(positions, width_all):
    half_width = width_all // 2
    freqs = THETA ** (-(2.0 * jnp.arange(half_width, dtype=jnp.float32)) / width_all)
    angles = positions.astype(jnp.float32)[..., None] * freqs
    angles = jnp.concatenate([angles, angles], -1)
    return (jnp.cos(angles), jnp.sin(angles))


def rotate(values, cosine_table, sine_table):
    half_width = values.shape[-1] // 2
    turned = jnp.concatenate([-values[..., half_width:], values[..., :half_width]], -1)
    return values * cosine_table + turned * sine_table


def head_prepare(projected, gain_row, cosine_table, sine_table, head_count):
    shaped = projected.reshape(projected.shape[:-1] + (head_count, gain_row.shape[0]))
    normed = rms_scale(shaped, gain_row)
    return rotate(normed, cosine_table[..., None, :], sine_table[..., None, :])


def forward_product(acts_in, weight_in):
    return jnp.einsum("bti,io->bto", acts_in, weight_in, preferred_element_type=jnp.float32)


def back_product(grads_in, weight_in):
    return jnp.einsum("bto,io->bti", grads_in, weight_in, preferred_element_type=jnp.float32)


def row_product(left_in, right_in):
    return jnp.einsum("bti,bto->io", left_in, right_in, preferred_element_type=jnp.float32)


def attend_scores(grouped_heads, key_row_matrix, visible, scale_by):
    raw = (
        jnp.einsum(
            "btkgd,bskd->bkgts", grouped_heads, key_row_matrix, preferred_element_type=jnp.float32
        )
        * scale_by
    )
    return jnp.where(visible[:, None, None, :, :], raw, -1e30)


def on_device(
    tokens,
    doc_ids,
    w_query,
    key_weight,
    value_weight,
    w_output,
    w_gate,
    w_up,
    w_down,
    norm_gains,
    head_norm_gains,
    out_grad,
):
    batch_rows, local_len, model_dim = tokens.shape
    head_dim = head_norm_gains.shape[1]
    kv_heads = key_weight.shape[1] // head_dim
    q_heads = w_query.shape[1] // head_dim
    group_size = q_heads // kv_heads
    scale_by = 1.0 / math.sqrt(head_dim)
    shard_width = norm_gains.shape[1]
    ff_width = w_gate.shape[1]
    full_ids = lax.all_gather(doc_ids, "ctx", axis=1, tiled=True)
    full_len = full_ids.shape[1]
    offset = lax.axis_index("ctx") * local_len
    query_index = offset + jnp.arange(local_len, dtype=jnp.int32)
    key_index = jnp.arange(full_len, dtype=jnp.int32)
    earlier = jnp.sum((full_ids[:, None, :] < doc_ids[:, :, None]).astype(jnp.int32), -1)
    positions = query_index[None, :] - earlier
    visible = (full_ids[:, None, :] == doc_ids[:, :, None]) & (
        key_index[None, None, :] <= query_index[None, :, None]
    )
    cosine_table, sine_table = rope_tables(positions, head_dim)
    attn_weights = (
        lax.all_gather(w_query, ("dp", "ctx"), axis=0, tiled=True),
        lax.all_gather(key_weight, ("dp", "ctx"), axis=0, tiled=True),
        lax.all_gather(value_weight, ("dp", "ctx"), axis=0, tiled=True),
        lax.all_gather(w_output, ("dp", "ctx"), axis=1, tiled=True),
        lax.all_gather(norm_gains, ("dp", "ctx"), axis=1, tiled=True),
    )
    wq_all, wk_all, wv_all, wo_all, gains_all = attn_weights
    gains_full = gains_all.astype(jnp.float32)
    head_full = head_norm_gains.astype(jnp.float32)
    inputs = tokens.astype(jnp.float32)
    normed_one = rms_scale(inputs, gains_full[0]).astype(jnp.bfloat16)
    q_pre = forward_product(normed_one, wq_all)
    key_before_norm = forward_product(normed_one, wk_all)
    value_own = forward_product(normed_one, wv_all).astype(jnp.bfloat16)
    query_rows = head_prepare(q_pre, head_full[0], cosine_table, sine_table, q_heads).astype(
        jnp.bfloat16
    )
    key_own = head_prepare(
        key_before_norm, head_full[1], cosine_table, sine_table, kv_heads
    ).astype(jnp.bfloat16)
    key_own = key_own.reshape(batch_rows, local_len, kv_heads * head_dim)
    key_row_matrix, value_row_matrix = (
        lax.all_gather(key_own, "ctx", axis=1, tiled=True),
        lax.all_gather(value_own, "ctx", axis=1, tiled=True),
    )
    key_row_matrix = key_row_matrix.reshape(batch_rows, full_len, kv_heads, head_dim)
    value_row_matrix = value_row_matrix.reshape(batch_rows, full_len, kv_heads, head_dim)
    grouped_heads = query_rows.reshape(batch_rows, local_len, kv_heads, group_size, head_dim)
    scores = attend_scores(grouped_heads, key_row_matrix, visible, scale_by)
    top_row = jnp.max(scores, -1, keepdims=True)
    expd = jnp.exp(scores - top_row)
    total_row = jnp.sum(expd, -1, keepdims=True)
    probs = expd / total_row
    log_total = top_row + jnp.log(total_row)
    mixed = jnp.einsum(
        "bkgts,bskd->btkgd",
        probs.astype(jnp.bfloat16),
        value_row_matrix,
        preferred_element_type=jnp.float32,
    )
    attn_out = mixed.reshape(batch_rows, local_len, q_heads * head_dim).astype(jnp.bfloat16)
    resid = inputs + forward_product(attn_out, wo_all)
    mlp_weights = (
        lax.all_gather(w_gate, ("dp", "ctx"), axis=0, tiled=True),
        lax.all_gather(w_up, ("dp", "ctx"), axis=0, tiled=True),
        lax.all_gather(w_down, ("dp", "ctx"), axis=1, tiled=True),
    )
    wg_all, wu_all, wd_all = mlp_weights
    normed_two = rms_scale(resid, gains_full[1]).astype(jnp.bfloat16)
    gate_act = forward_product(normed_two, wg_all)
    up_act = forward_product(normed_two, wu_all)
    hidden = (jax.nn.silu(gate_act) * up_act).astype(jnp.bfloat16)
    layer_out = (resid + forward_product(hidden, wd_all)).astype(jnp.bfloat16)
    mlp_back = (
        lax.all_gather(w_gate, ("dp", "ctx"), axis=0, tiled=True),
        lax.all_gather(w_up, ("dp", "ctx"), axis=0, tiled=True),
        lax.all_gather(w_down, ("dp", "ctx"), axis=1, tiled=True),
    )
    wg_back, wu_back, wd_back = mlp_back
    grad_hidden = back_product(out_grad, wd_back)
    _, gate_pull = jax.vjp(lambda gate_in, up_in: jax.nn.silu(gate_in) * up_in, gate_act, up_act)
    grad_gate_full, grad_up_full = gate_pull(grad_hidden)
    grad_gate_low = grad_gate_full.astype(jnp.bfloat16)
    grad_up_low = grad_up_full.astype(jnp.bfloat16)
    grad_norm_two = back_product(grad_gate_low, wg_back) + back_product(grad_up_low, wu_back)
    _, second_pull = jax.vjp(rms_scale, resid, gains_full[1])
    grad_resid_norm, grad_gain_two = second_pull(grad_norm_two)
    grad_resid = out_grad.astype(jnp.float32) + grad_resid_norm
    gate_up_low = jnp.concatenate([grad_gate_low, grad_up_low], 2)
    normed_cols = normed_two
    grad_cols = out_grad
    first_part = row_product(normed_cols, gate_up_low)
    second_part = row_product(grad_cols, hidden)
    mlp_sums = lax.psum_scatter(
        jnp.concatenate([first_part, second_part], 1),
        ("dp", "ctx"),
        scatter_dimension=0,
        tiled=True,
    )
    attn_back = (
        lax.all_gather(w_query, ("dp", "ctx"), axis=0, tiled=True),
        lax.all_gather(key_weight, ("dp", "ctx"), axis=0, tiled=True),
        lax.all_gather(value_weight, ("dp", "ctx"), axis=0, tiled=True),
        lax.all_gather(w_output, ("dp", "ctx"), axis=1, tiled=True),
    )
    wq_back, wk_back, wv_back, wo_back = attn_back
    grad_attn_low = grad_resid.astype(jnp.bfloat16)
    grad_mixed = back_product(grad_attn_low, wo_back).astype(jnp.bfloat16)
    grad_grouped = grad_mixed.reshape(batch_rows, local_len, kv_heads, group_size, head_dim)
    scores = attend_scores(grouped_heads, key_row_matrix, visible, scale_by)
    probs = jnp.exp(scores - log_total)
    grad_probs = jnp.einsum(
        "btkgd,bskd->bkgts", grad_grouped, value_row_matrix, preferred_element_type=jnp.float32
    )
    value_part = jnp.einsum(
        "bkgts,btkgd->bskd",
        probs.astype(jnp.bfloat16),
        grad_grouped,
        preferred_element_type=jnp.float32,
    )
    inner_row = jnp.sum(probs * grad_probs, -1, keepdims=True)
    grad_scores = (probs * (grad_probs - inner_row)).astype(jnp.bfloat16)
    grad_queries = (
        jnp.einsum(
            "bkgts,bskd->btkgd", grad_scores, key_row_matrix, preferred_element_type=jnp.float32
        )
        * scale_by
    )
    key_part = (
        jnp.einsum(
            "bkgts,btkgd->bskd", grad_scores, grouped_heads, preferred_element_type=jnp.float32
        )
        * scale_by
    )
    key_sum, value_sum = (
        lax.psum_scatter(
            key_part.reshape(batch_rows, full_len, kv_heads * head_dim).astype(jnp.bfloat16),
            "ctx",
            scatter_dimension=1,
            tiled=True,
        ).astype(jnp.float32),
        lax.psum_scatter(
            value_part.reshape(batch_rows, full_len, kv_heads * head_dim).astype(jnp.bfloat16),
            "ctx",
            scatter_dimension=1,
            tiled=True,
        ).astype(jnp.float32),
    )
    _, query_pull = jax.vjp(
        lambda proj_in, gain_in: head_prepare(proj_in, gain_in, cosine_table, sine_table, q_heads),
        q_pre,
        head_full[0],
    )
    grad_q_pre, grad_q_gain = query_pull(
        grad_queries.reshape(batch_rows, local_len, q_heads, head_dim)
    )
    _, key_pull = jax.vjp(
        lambda proj_in, gain_in: head_prepare(proj_in, gain_in, cosine_table, sine_table, kv_heads),
        key_before_norm,
        head_full[1],
    )
    grad_k_pre, grad_k_gain = key_pull(key_sum.reshape(batch_rows, local_len, kv_heads, head_dim))
    grad_q_low = grad_q_pre.astype(jnp.bfloat16)
    grad_k_low = grad_k_pre.astype(jnp.bfloat16)
    grad_v_low = value_sum.astype(jnp.bfloat16)
    grad_norm_one = (
        back_product(grad_q_low, wq_back)
        + back_product(grad_k_low, wk_back)
        + back_product(grad_v_low, wv_back)
    )
    _, first_pull = jax.vjp(rms_scale, inputs, gains_full[0])
    grad_input_norm, grad_gain_one = first_pull(grad_norm_one)
    input_grad = (grad_resid + grad_input_norm).astype(jnp.bfloat16)
    qkv_low = jnp.concatenate([grad_q_low, grad_k_low, grad_v_low], 2)
    normed_cols = normed_one
    grad_cols = grad_attn_low
    first_part = row_product(normed_cols, qkv_low)
    second_part = row_product(grad_cols, attn_out)
    attn_sums = lax.psum_scatter(
        jnp.concatenate([first_part, second_part], 1),
        ("dp", "ctx"),
        scatter_dimension=0,
        tiled=True,
    )
    norm_total, head_sum = lax.psum(
        (jnp.stack([grad_gain_one, grad_gain_two]), jnp.stack([grad_q_gain, grad_k_gain])),
        ("dp", "ctx"),
    )
    norm_own = lax.dynamic_slice_in_dim(
        norm_total, lax.axis_index(("dp", "ctx")) * shard_width, shard_width, 1
    )
    q_cols = q_heads * head_dim
    kv_cols = kv_heads * head_dim
    grad_q_out = attn_sums[:, :q_cols]
    grad_k_out = attn_sums[:, q_cols : q_cols + kv_cols]
    grad_v_out = attn_sums[:, q_cols + kv_cols : q_cols + 2 * kv_cols]
    grad_o_out = attn_sums[:, q_cols + 2 * kv_cols :].T
    grad_g_out = mlp_sums[:, :ff_width]
    grad_u_out = mlp_sums[:, ff_width : 2 * ff_width]
    grad_d_out = mlp_sums[:, 2 * ff_width :].T
    return (
        layer_out,
        input_grad,
        grad_q_out.astype(jnp.bfloat16),
        grad_k_out.astype(jnp.bfloat16),
        grad_v_out.astype(jnp.bfloat16),
        grad_o_out.astype(jnp.bfloat16),
        grad_g_out.astype(jnp.bfloat16),
        grad_u_out.astype(jnp.bfloat16),
        grad_d_out.astype(jnp.bfloat16),
        norm_own.astype(jnp.bfloat16),
        head_sum.astype(jnp.bfloat16),
    )


def solution(mesh):
    in_specs = (
        P("dp", "ctx", None),
        P("dp", "ctx"),
        P(("dp", "ctx"), None),
        P(("dp", "ctx"), None),
        P(("dp", "ctx"), None),
        P(None, ("dp", "ctx")),
        P(("dp", "ctx"), None),
        P(("dp", "ctx"), None),
        P(None, ("dp", "ctx")),
        P(None, ("dp", "ctx")),
        P(),
        P("dp", "ctx", None),
    )
    out_specs = (
        P("dp", "ctx", None),
        P("dp", "ctx", None),
        P(("dp", "ctx"), None),
        P(("dp", "ctx"), None),
        P(("dp", "ctx"), None),
        P(None, ("dp", "ctx")),
        P(("dp", "ctx"), None),
        P(("dp", "ctx"), None),
        P(None, ("dp", "ctx")),
        P(None, ("dp", "ctx")),
        P(),
    )
    return jax.shard_map(
        on_device, mesh=mesh, in_specs=in_specs, out_specs=out_specs, check_vma=False
    )
```

profile of v0, /device:TPU:0, one launch (start us, length us, event | category | flops | bytes accessed | tf_op | source)
XLA Modules:
  0.0 1282.6 jit_solution(11986059762425611412)
XLA Ops:
  9.4 43.2 %all-gather.2 = bf16[32,32,2]{1,2,0:T(2,128)(2,1)S(1)} all-gather(bf16[1,32,2]{1,2,0:T(2,128)(2,1)} %bitcast.272), channel_id=1, replica_groups=mesh['dp'=8,'ctx'=4] {'dp','ctx'}, dimensions={0}, use_global_device_ids=true | all-gather | bytes 4224 | tf_op jit(solution)/shard_map/all_gather | solution.py:96
  71.0 51.8 %all-gather.15.cloned.1.call-done = bf16[1024,512]{1,0:T(8,128)(2,1)} async-done(((bf16[32,512]{1,0:T(8,128)(2,1)}), bf16[1024,512]{1,0:T(8,128)(2,1)}) %all-gather.15.cloned.1.call-update) | async-done | bytes 1048592 | tf_op jit(solution)/shard_map/all_gather | solution.py:93
  142.9 16.5 %all-gather.29.cloned.1.call-done = bf16[1024,512]{1,0:T(8,128)(2,1)} async-done(((bf16[256,512]{1,0:T(8,128)(2,1)}), bf16[1024,512]{1,0:T(8,128)(2,1)}) %all-gather.29.cloned.1.call-update) | async-done | bytes 1048592 | tf_op jit(solution)/shard_map/all_gather | solution.py:114
  160.9 57.6 %all-gather.17.cloned.1.call-done = bf16[1024,1024]{1,0:T(8,128)(2,1)} async-done(((bf16[32,1024]{1,0:T(8,128)(2,1)}), bf16[1024,1024]{1,0:T(8,128)(2,1)}) %all-gather.17.cloned.1.call-update) | async-done | bytes 2097168 | tf_op jit(solution)/shard_map/all_gather | solution.py:92
  231.3 8.1 fusion.3
  239.4 7.3 fusion.24
  246.7 29.7 %all-gather.19.cloned.1.call-done = bf16[1024,1024]{0,1:T(8,128)(2,1)} async-done(((bf16[1024,32]{0,1:T(8,128)(2,1)}), bf16[1024,1024]{0,1:T(8,128)(2,1)}) %all-gather.19.cloned.1.call-update) | async-done | bytes 2097168 | tf_op jit(solution)/shard_map/all_gather | solution.py:95
  279.8 80.5 %all-gather.23.cloned.1.call-done = bf16[1024,4608]{1,0:T(8,128)(2,1)} async-done(((bf16[32,4608]{1,0:T(8,128)(2,1)}), bf16[1024,4608]{1,0:T(8,128)(2,1)}) %all-gather.23.cloned.1.call-update) | async-done | bytes 9437200 | tf_op jit(solution)/shard_map/all_gather | solution.py:136
  360.3 7.9 fusion.84
  368.2 75.7 %all-gather.21.cloned.1.call-done = bf16[1024,4608]{1,0:T(8,128)(2,1)} async-done(((bf16[32,4608]{1,0:T(8,128)(2,1)}), bf16[1024,4608]{1,0:T(8,128)(2,1)}) %all-gather.21.cloned.1.call-update) | async-done | bytes 9437200 | tf_op jit(solution)/shard_map/all_gather | solution.py:135
  443.9 7.9 fusion.83
  451.8 75.6 %all-gather.25.cloned.1.call-done = bf16[4608,1024]{0,1:T(8,128)(2,1)} async-done(((bf16[4608,32]{0,1:T(8,128)(2,1)}), bf16[4608,1024]{0,1:T(8,128)(2,1)}) %all-gather.25.cloned.1.call-update) | async-done | bytes 9437200 | tf_op jit(solution)/shard_map/all_gather | solution.py:137
  527.5 10.7 multiply_convert_fusion
  550.1 16.3 %fusion = (f32[8,2,256]{2,1,0:T(2,128)}, f32[8,1024,256,2]{2,1,3,0:T(8,128)}) fusion(f32[1,8,2,256,1024]{3,4,2,1,0:T(8,128)} %get-tuple-element.47, f32[8,2,256]{2,1,0:T(2,128)} %bitcast.249, bf16[1024,8,64,1]{0,2,3,1:T(8,128)(2,1)} %bitcast.233, bf16[256,8,2,64]{0,3,2,1:T(8,128)(2,1)} %bitcast.229), kind=kOutput, calls=%fused_computation.4 | convolution fusion | flops 549449728 | bytes 35160064 | tf_op jit(solution)/shard_map/btkgd,bskd->bkgts/dot_general | solution.py:183
  566.5 7.6 fusion.8
  584.3 9.8 bitcast_convert_fusion
  605.3 23.7 %reduce-scatter.7.cloned.1.call-done = bf16[1,256,512]{1,2,0:T(8,128)(2,1)} async-done(((bf16[1,1024,512]{1,2,0:T(8,128)(2,1)}), bf16[1,256,512]{1,2,0:T(8,128)(2,1)}) %reduce-scatter.7.cloned.1.call-update) | async-done | bytes 262160 | tf_op jit(solution)/shard_map/reduce_scatter | solution.py:213
  637.6 19.4 %fusion.15 = f32[1024,9216]{1,0:T(8,128)} fusion(bf16[256,1024]{1,0:T(8,128)(2,1)S(1)} %copy-done.17, bf16[1,256,4608]{2,1,0:T(8,128)(2,1)} %bitcast.238, bf16[1,256,4608]{2,1,0:T(8,128)(2,1)} %bitcast.239), kind=kOutput, calls=%fused_computation.25 | convolution fusion | flops 4841275392 | bytes 42991616 | tf_op jit(solution)/shard_map/bti,bto->io/dot_general | solution.py:45
  657.0 8.6 convolution_bitcast_fusion
  665.5 39.1 %pad_maximum_fusion = f32[1024,13824]{1,0:T(8,128)} fusion(f32[1024,4608]{1,0:T(8,128)} %convolution_bitcast_fusion, f32[1024,9216]{1,0:T(8,128)} %fusion.15), kind=kLoop, calls=%fused_computation | loop fusion | flops 14155776 | bytes 113246208 | tf_op jit(solution)/shard_map/concatenate | solution.py:166
  707.1 8.1 fusion.23
  716.6 40.9 %all-reduce.4 = (bf16[2,1024]{1,0:T(2,128)(2,1)S(1)}, bf16[2,64]{1,0:T(2,128)(2,1)}) all-reduce(f32[2,1024]{1,0:T(2,128)S(1)} %pad_maximum_fusion.4, f32[2,64]{1,0:T(2,128)S(1)} %pad_maximum_fusion.5), channel_id=1, replica_groups=mesh['dp'=8,'ctx'=4] {'dp','ctx'}, use_global_device_ids=true, to_apply=%region_18.19 | all-reduce | flops 2176 | bytes 13056 | tf_op jit(solution)/shard_map/psum | solution.py:256
  759.2 33.9 %reduce-scatter.9.cloned.1.call-done = f32[32,3072]{1,0:T(8,128)} async-done(((f32[1024,3072]{1,0:T(8,128)}), f32[32,3072]{1,0:T(8,128)}) %reduce-scatter.9.cloned.1.call-update) | async-done | bytes 393232 | tf_op jit(solution)/shard_map/reduce_scatter | solution.py:250
  795.4 477.9 %reduce-scatter.11.cloned.1.call-done = f32[32,13824]{1,0:T(8,128)} async-done(((f32[1024,13824]{1,0:T(8,128)}), f32[32,13824]{1,0:T(8,128)}) %reduce-scatter.11.cloned.1.call-update) | async-done | bytes 1769488 | tf_op jit(solution)/shard_map/reduce_scatter | solution.py:165
  (229 shorter events, 109.5 us)
Async XLA Ops:
  7.2 60.1 %all-gather.13.cloned.1.call-start = ((), (), s32[]{:S(2)}) async-start(), calls=%async_computation.4 | async-start | bytes 1081344 | tf_op jit(solution)/shard_map/all_gather | solution.py:94
  7.9 114.9 %all-gather.15.cloned.1.call-start = ((), (), s32[]{:S(2)}) async-start(), calls=%async_computation.5 | async-start | bytes 1081344 | tf_op jit(solution)/shard_map/all_gather | solution.py:93
  8.7 132.0 %all-gather.27.cloned.1.call-start = ((), (), s32[]{:S(2)}) async-start(), calls=%async_computation.15 | async-start | bytes 1310720 | tf_op jit(solution)/shard_map/all_gather | solution.py:115
  60.6 71.5 %copy-start.48 = (f32[64]{0:T(128)}, f32[64]{0:T(128)S(1)}, u32[]{:S(2)}) copy-start(f32[64]{0:T(128)S(1)} %get-tuple-element.45) | copy-start | bytes 772
  69.9 89.5 %all-gather.29.cloned.1.call-start = ((), (), s32[]{:S(2)}) async-start(), calls=%async_computation.16 | async-start | bytes 1310720 | tf_op jit(solution)/shard_map/all_gather | solution.py:114
  70.1 152.7 %copy-start.22 = (f32[256,64]{0,1:T(8,128)}, f32[256,64]{0,1:T(8,128)S(1)}, u32[]{:S(2)}) copy-start(f32[256,64]{0,1:T(8,128)S(1)} %get-tuple-element.40) | copy-start | bytes 196612
  70.2 65.9 %copy-start.52 = (s32[1,256]{1,0:T(1,128)S(1)}, s32[1,256]{1,0:T(1,128)}, u32[]{:S(2)}) copy-start(s32[1,256]{1,0:T(1,128)} %param.13) | copy-start | bytes 3076
  124.7 93.8 %copy-start.1 = (bf16[1,256,1024]{2,1,0:T(8,128)(2,1)S(1)}, bf16[1,256,1024]{2,1,0:T(8,128)(2,1)}, u32[]{:S(2)}) copy-start(bf16[1,256,1024]{2,1,0:T(8,128)(2,1)} %param.12) | copy-start | bytes 1572868
  132.2 90.7 %copy-start.30 = (f32[256,64]{0,1:T(8,128)S(1)}, f32[256,64]{0,1:T(8,128)}, u32[]{:S(2)}) copy-start(f32[256,64]{0,1:T(8,128)} %copy-done.29) | copy-start | bytes 196612
  132.2 90.7 %copy-start.46 = (f32[64]{0:T(128)S(1)}, f32[64]{0:T(128)}, u32[]{:S(2)}) copy-start(f32[64]{0:T(128)} %get-tuple-element.44) | copy-start | bytes 772
  132.2 86.3 %all-gather.17.cloned.1.call-start = ((), (), s32[]{:S(2)}) async-start(), calls=%async_computation.6 | async-start | bytes 2162688 | tf_op jit(solution)/shard_map/all_gather | solution.py:92
  132.8 143.7 %all-gather.19.cloned.1.call-start = ((), (), s32[]{:S(2)}) async-start(), calls=%async_computation.7 | async-start | bytes 2162688 | tf_op jit(solution)/shard_map/all_gather | solution.py:95
  133.4 227.0 %all-gather.23.cloned.1.call-start = ((), (), s32[]{:S(2)}) async-start(), calls=%async_computation.9 | async-start | bytes 9732096 | tf_op jit(solution)/shard_map/all_gather | solution.py:136
  134.1 309.8 %all-gather.21.cloned.1.call-start = ((), (), s32[]{:S(2)}) async-start(), calls=%async_computation.8 | async-start | bytes 9732096 | tf_op jit(solution)/shard_map/all_gather | solution.py:135
  134.9 392.6 %all-gather.25.cloned.1.call-start = ((), (), s32[]{:S(2)}) async-start(), calls=%async_computation.10 | async-start | bytes 9732096 | tf_op jit(solution)/shard_map/all_gather | solution.py:137
  135.6 466.3 %reduce-scatter.5.cloned.1.call-start = ((), (), s32[]{:S(2)}) async-start(), calls=%async_computation.11 | async-start | bytes 1310720 | tf_op jit(solution)/shard_map/reduce_scatter | solution.py:207
  160.9 70.4 %copy-start.6 = (bf16[1024,512]{0,1:T(8,128)(2,1)}, bf16[1024,512]{0,1:T(8,128)(2,1)S(1)}, u32[]{:S(2)}) copy-start(bf16[1024,512]{0,1:T(8,128)(2,1)S(1)} %copy.107) | copy-start | bytes 3145732
  246.7 121.5 %copy-start.26 = (bf16[8,64,2,256]{3,1,2,0:T(8,128)(2,1)}, bf16[8,64,2,256]{3,1,2,0:T(8,128)(2,1)S(1)}, u32[]{:S(2)}) copy-start(bf16[8,64,2,256]{3,1,2,0:T(8,128)(2,1)S(1)} %fusion.24) | copy-start | bytes 1572868
  278.9 268.2 %copy-start.14 = (f32[1,256,1024]{2,1,0:T(8,128)}, f32[1,256,1024]{2,1,0:T(8,128)S(1)}, u32[]{:S(2)}) copy-start(f32[1,256,1024]{2,1,0:T(8,128)S(1)} %get-tuple-element.49) | copy-start | bytes 3145732
  279.8 172.0 %copy-start.16 = (bf16[256,1024]{1,0:T(8,128)(2,1)}, bf16[256,1024]{1,0:T(8,128)(2,1)S(1)}, u32[]{:S(2)}) copy-start(bf16[256,1024]{1,0:T(8,128)(2,1)S(1)} %fusion.52) | copy-start | bytes 1572868
  443.9 83.6 %copy-start.27 = (bf16[1,256,1024]{2,1,0:T(8,128)(2,1)S(1)}, bf16[1,256,1024]{2,1,0:T(8,128)(2,1)}, u32[]{:S(2)}) copy-start(bf16[1,256,1024]{2,1,0:T(8,128)(2,1)} %param.23) | copy-start | bytes 1572868
  577.8 51.3 %reduce-scatter.7.cloned.1.call-start = ((), (), s32[]{:S(2)}) async-start(), calls=%async_computation.12 | async-start | bytes 1310720 | tf_op jit(solution)/shard_map/reduce_scatter | solution.py:213
  594.1 198.9 %reduce-scatter.9.cloned.1.call-start = ((), (), s32[]{:S(2)}) async-start(), calls=%async_computation.13 | async-start | bytes 12976128 | tf_op jit(solution)/shard_map/reduce_scatter | solution.py:250
  636.6 636.7 %reduce-scatter.11.cloned.1.call-start = ((), (), s32[]{:S(2)}) async-start(), calls=%async_computation.14 | async-start | bytes 58392576 | tf_op jit(solution)/shard_map/reduce_scatter | solution.py:165
  (48 other events, 644.6 us)
Sparse Core Ops, SparseCore 0:
  10.9 56.3 all-gather.12
  70.1 52.6 all-gather.14
  124.9 15.6 all-gather.26
  142.6 16.7 all-gather.28
  162.1 56.3 all-gather.16
  221.2 55.2 all-gather.18
  279.4 80.8 all-gather.22
  363.2 80.6 all-gather.20
  446.8 80.6 all-gather.24
  577.9 23.4 reduce-scatter.4
  604.1 24.9 reduce-scatter.6
  636.7 156.3 reduce-scatter.8
  800.6 472.6 reduce-scatter.10
where the time goes:
time: 1290 us; the launch traced here: 1280 us
  waiting for transfers between devices  938 us (73%)
  matrix products  141 us (11%)
  blocking collectives  89.4 us (7%)
  other arithmetic  81.5 us (6%)
  local copies, waits for them, and re-layouts  16.4 us (1%)
  between operations  15.1 us (1%)
    reduce_scatter x2, waiting for transfers between devices, on_device(): lax.psum_scatter(jnp.concatenate([first_part, second_part], 1), ('dp', 'c...  512 us
    all_gather x1, waiting for transfers between devices, on_device(): lax.all_gather(w_up, ('dp', 'ctx'), axis=0, tiled=True)  80.5 us
    all_gather x1, waiting for transfers between devices, on_device(): lax.all_gather(w_gate, ('dp', 'ctx'), axis=0, tiled=True)  75.7 us
    all_gather x1, waiting for transfers between devices, on_device(): lax.all_gather(w_down, ('dp', 'ctx'), axis=1, tiled=True)  75.6 us
    all_gather x1, waiting for transfers between devices, on_device(): lax.all_gather(w_query, ('dp', 'ctx'), axis=0, tiled=True)  57.6 us
    all_gather x1, waiting for transfers between devices, on_device(): lax.all_gather(key_weight, ('dp', 'ctx'), axis=0, tiled=True)  51.8 us
    concatenate x2, other arithmetic, on_device(): jnp.concatenate([first_part, second_part], 1)  43.9 us
    all_gather x1, blocking collectives, on_device(): lax.all_gather(norm_gains, ('dp', 'ctx'), axis=1, tiled=True)  43.2 us
  transfers between devices with their start and end apart: 13, of which 12 were waited for; matrix products, arithmetic and copies ran while one was open for 14% of the time, Pallas kernels for 0%

commit v1 on v0

v1 whole, which is shorter than its diff:
```python
import math

import jax
import jax.numpy as jnp
from jax import lax
from jax.sharding import PartitionSpec as P

EPS = 1e-05
THETA = 1000000.0
BF = jnp.bfloat16
F32 = jnp.float32
ALL = ("dp", "ctx")


def add_low(a, b):
    return (a.astype(F32) + b.astype(F32)).astype(BF)


def flip(value, axis, size, bits):
    return lax.ppermute(value, axis, [(i, i ^ bits) for i in range(size)])


def gather_ctx(own):
    core = flip(own, "ctx", 4, 1)
    across = flip(own, "ctx", 4, 2)
    return [own, core, across, flip(across, "ctx", 4, 1)]


def scatter_ctx(parts):
    far = flip(parts[3], "ctx", 4, 1)
    near = flip(parts[1], "ctx", 4, 1)
    far_sum = add_low(parts[2], far)
    far_in = flip(far_sum, "ctx", 4, 2)
    return parts[0].astype(F32) + near.astype(F32) + far_in.astype(F32)


def exchange_ctx(parts):
    return [parts[0]] + [flip(parts[j], "ctx", 4, j) for j in range(1, 4)]


def place(parts, where, axis):
    size = parts[0].shape[axis]
    shape = list(parts[0].shape)
    shape[axis] = size * len(parts)
    out = jnp.zeros(shape, parts[0].dtype)
    for part, at in zip(parts, where):
        out = lax.dynamic_update_slice_in_dim(out, part, at * size, axis)
    return out


def ring(value, size):
    return lax.ppermute(value, "dp", [(i, (i + 2) % size) for i in range(size)])


def gather_dp(block, size):
    if size < 4 or size > 8:
        return lax.all_gather(block, "dp", axis=0, tiled=True)
    me = lax.axis_index("dp")
    parts, where = [], []
    for step in range(size // 2):
        at = (me - 2 * step) % size
        parts += [block, flip(block, "dp", size, 1)]
        where += [at, at ^ 1]
        if step + 1 < size // 2:
            block = ring(block, size)
    return place(parts, where, 0)


def scatter_dp(whole, size):
    if size < 4 or size > 8:
        return lax.psum_scatter(whole, "dp", scatter_dimension=0, tiled=True).astype(F32)
    me = lax.axis_index("dp")
    rows = whole.shape[0] // size

    def part(at):
        return lax.dynamic_slice_in_dim(whole, at * rows, rows, 0)

    total = None
    for step in range(size // 2):
        at = (me - 2 * (step + 1)) % size
        near = flip(part(at ^ 1), "dp", size, 1)
        own = part(at).astype(F32) + near.astype(F32)
        if total is not None:
            own = own + ring(total, size).astype(F32)
        total = own.astype(BF)
    return own


def sum_all(value, dp_size):
    for bits in (1, 2):
        value = value + flip(value, "ctx", 4, bits)
    bits = 1
    while bits < dp_size:
        value = value + flip(value, "dp", dp_size, bits)
        bits *= 2
    return value


def dot(a, b):
    return lax.dot_general(a, b, (((1,), (0,)), ((), ())), preferred_element_type=F32)


def dot_nt(a, b):
    return lax.dot_general(a, b, (((1,), (1,)), ((), ())), preferred_element_type=F32)


def dot_tn(a, b):
    return lax.dot_general(a, b, (((0,), (0,)), ((), ())), preferred_element_type=F32)


def rms_scale(values, gain_row):
    return values * lax.rsqrt(jnp.mean(values * values, -1, keepdims=True) + EPS) * gain_row


def rope_tables(positions, width_all):
    half_width = width_all // 2
    freqs = THETA ** (-(2.0 * jnp.arange(half_width, dtype=jnp.float32)) / width_all)
    angles = positions.astype(jnp.float32)[..., None] * freqs
    angles = jnp.concatenate([angles, angles], -1)
    return (jnp.cos(angles), jnp.sin(angles))


def rotate(values, cosine_table, sine_table):
    half_width = values.shape[-1] // 2
    turned = jnp.concatenate([-values[..., half_width:], values[..., :half_width]], -1)
    return values * cosine_table + turned * sine_table


def head_prepare(projected, gain_row, cosine_table, sine_table, head_count):
    shaped = projected.reshape(projected.shape[:-1] + (head_count, gain_row.shape[0]))
    normed = rms_scale(shaped, gain_row)
    return rotate(normed, cosine_table[..., None, :], sine_table[..., None, :])


def split_parts(tall, count):
    rows = tall.shape[0] // count
    return [lax.slice_in_dim(tall, j * rows, (j + 1) * rows, axis=0) for j in range(count)]


def on_device(
    dp_size,
    tokens,
    doc_ids,
    w_query,
    key_weight,
    value_weight,
    w_output,
    w_gate,
    w_up,
    w_down,
    norm_gains,
    head_norm_gains,
    out_grad,
):
    local_len, model_dim = tokens.shape[1:]
    tokens, out_grad, doc_row = tokens[0], out_grad[0], doc_ids[0]
    head_dim = head_norm_gains.shape[1]
    q_cols, kv_cols = w_query.shape[1] // 4, key_weight.shape[1] // 4
    q_heads, kv_heads = q_cols // head_dim, kv_cols // head_dim
    group_size = q_heads // kv_heads
    scale_by = 1.0 / math.sqrt(head_dim)
    shard = norm_gains.shape[1]
    ff_cols = w_gate.shape[1] // 4
    me = lax.axis_index("ctx")
    places = [me ^ j for j in range(4)]

    def spread(pieces):
        sent = []
        for at in places:
            cut = [
                lax.dynamic_slice_in_dim(p, at * (p.shape[1] // 4), p.shape[1] // 4, 1)
                for p in pieces
            ]
            sent.append(jnp.concatenate(cut, 1))
        block = place(exchange_ctx(sent), places, 0)
        return gather_dp(block, dp_size)

    gains_full = lax.all_gather(norm_gains, ALL, axis=1, tiled=True).astype(F32)
    attn_w = spread([w_query, key_weight, value_weight, w_output.T])
    wq = attn_w[:, :q_cols]
    wk = attn_w[:, q_cols : q_cols + kv_cols]
    wv = attn_w[:, q_cols + kv_cols : q_cols + 2 * kv_cols]
    wo_t = attn_w[:, q_cols + 2 * kv_cols :]
    wg = spread([w_gate])
    wu = spread([w_up])
    wd_t = spread([w_down.T])

    head_full = head_norm_gains.astype(F32)
    docs = jnp.concatenate(gather_ctx(doc_row.reshape(1, -1)), 1)[0]
    all_tokens = jnp.concatenate(gather_ctx(tokens), 0)
    all_grad = jnp.concatenate(gather_ctx(out_grad), 0)
    index = jnp.concatenate(
        [at * local_len + jnp.arange(local_len, dtype=jnp.int32) for at in places]
    )
    earlier = jnp.sum((docs[None, :] < docs[:, None]).astype(jnp.int32), -1)
    positions = index - earlier
    visible = (docs[None, :] == docs[:, None]) & (index[None, :] <= index[:, None])
    cosine_table, sine_table = rope_tables(positions, head_dim)

    inputs = all_tokens.astype(F32)
    normed_one = rms_scale(inputs, gains_full[0]).astype(BF)
    q_pre = dot(normed_one, wq)
    k_pre = dot(normed_one, wk)
    value_rows = dot(normed_one, wv).astype(BF)
    query_rows = head_prepare(q_pre, head_full[0], cosine_table, sine_table, q_heads).astype(BF)
    key_rows = head_prepare(k_pre, head_full[1], cosine_table, sine_table, kv_heads).astype(BF)
    value_rows = value_rows.reshape(-1, kv_heads, head_dim)
    grouped = query_rows.reshape(-1, kv_heads, group_size, head_dim)

    def attend_scores():
        raw = (
            jnp.einsum("tkgd,skd->kgts", grouped, key_rows, preferred_element_type=F32) * scale_by
        )
        return jnp.where(visible[None, None], raw, -1e30)

    scores = attend_scores()
    top_row = jnp.max(scores, -1, keepdims=True)
    expd = jnp.exp(scores - top_row)
    total_row = jnp.sum(expd, -1, keepdims=True)
    probs = expd / total_row
    log_total = top_row + jnp.log(total_row)
    mixed = jnp.einsum(
        "kgts,skd->tkgd", probs.astype(BF), value_rows, preferred_element_type=F32
    )
    attn_out = mixed.reshape(-1, q_cols).astype(BF)
    resid_sum = scatter_ctx(split_parts(dot_nt(attn_out, wo_t).astype(BF), 4))
    resid = tokens.astype(F32) + resid_sum
    normed_own = rms_scale(resid, gains_full[1]).astype(BF)
    normed_two = jnp.concatenate(gather_ctx(normed_own), 0)

    gate_act = dot(normed_two, wg)
    up_act = dot(normed_two, wu)
    hidden = (jax.nn.silu(gate_act) * up_act).astype(BF)
    grad_hidden = dot(all_grad, wd_t)
    _, gate_pull = jax.vjp(lambda g, u: jax.nn.silu(g) * u, gate_act, up_act)
    grad_gate_full, grad_up_full = gate_pull(grad_hidden)
    grad_gate = grad_gate_full.astype(BF)
    grad_up = grad_up_full.astype(BF)
    grad_two_part = (dot_nt(grad_gate, wg) + dot_nt(grad_up, wu)).astype(BF)
    grad_norm_two = scatter_ctx(split_parts(grad_two_part, 4))
    _, second_pull = jax.vjp(rms_scale, resid, gains_full[1])
    grad_resid_norm, grad_gain_two = second_pull(grad_norm_two)
    grad_resid = out_grad.astype(F32) + grad_resid_norm
    down_part = dot_nt(hidden, wd_t).astype(BF)
    layer_out = (resid + scatter_ctx(split_parts(down_part, 4))).astype(BF)

    def collect(whole, widths):
        mine = scatter_dp(whole.astype(BF), dp_size).astype(BF)
        sent = [lax.dynamic_slice_in_dim(mine, at * shard, shard, 0) for at in places]
        got = exchange_ctx(sent)
        outs, start = [], 0
        for width in widths:
            cut = [g[:, start : start + width] for g in got]
            outs.append(place(cut, places, 1))
            start += width
        return outs

    (grad_g_out,) = collect(dot_tn(normed_two, grad_gate), (ff_cols,))
    (grad_u_out,) = collect(dot_tn(normed_two, grad_up), (ff_cols,))
    (grad_d_out,) = collect(dot_tn(all_grad, hidden), (ff_cols,))

    grad_attn = jnp.concatenate(gather_ctx(grad_resid.astype(BF)), 0)
    grad_mixed = dot(grad_attn, wo_t).astype(BF)
    grad_grouped = grad_mixed.reshape(-1, kv_heads, group_size, head_dim)
    probs = jnp.exp(attend_scores() - log_total)
    grad_probs = jnp.einsum(
        "tkgd,skd->kgts", grad_grouped, value_rows, preferred_element_type=F32
    )
    value_part = jnp.einsum(
        "kgts,tkgd->skd", probs.astype(BF), grad_grouped, preferred_element_type=F32
    )
    inner_row = jnp.sum(probs * grad_probs, -1, keepdims=True)
    grad_scores = (probs * (grad_probs - inner_row)).astype(BF)
    grad_queries = (
        jnp.einsum("kgts,skd->tkgd", grad_scores, key_rows, preferred_element_type=F32) * scale_by
    )
    grad_keys = (
        jnp.einsum("kgts,tkgd->skd", grad_scores, grouped, preferred_element_type=F32) * scale_by
    )
    _, query_pull = jax.vjp(
        lambda v, g: head_prepare(v, g, cosine_table, sine_table, q_heads), q_pre, head_full[0]
    )
    grad_q_pre, grad_q_gain = query_pull(grad_queries.reshape(-1, q_heads, head_dim))
    _, key_pull = jax.vjp(
        lambda v, g: head_prepare(v, g, cosine_table, sine_table, kv_heads), k_pre, head_full[1]
    )
    grad_k_pre, grad_k_gain = key_pull(grad_keys)
    grad_qkv = jnp.concatenate(
        [grad_q_pre.astype(BF), grad_k_pre.astype(BF), value_part.reshape(-1, kv_cols).astype(BF)],
        1,
    )
    w_qkv = attn_w[:, : q_cols + 2 * kv_cols]
    grad_one_part = dot_nt(grad_qkv, w_qkv)
    _, first_pull = jax.vjp(rms_scale, inputs, gains_full[0])
    grad_gain_one = first_pull(grad_one_part)[1]
    grad_norm_one = scatter_ctx(split_parts(grad_one_part.astype(BF), 4))
    _, own_pull = jax.vjp(rms_scale, tokens.astype(F32), gains_full[0])
    input_grad = (grad_resid + own_pull(grad_norm_one)[0]).astype(BF)
    grad_attn_w = jnp.concatenate([dot_tn(normed_one, grad_qkv), dot_tn(grad_attn, attn_out)], 1)
    grad_q_out, grad_k_out, grad_v_out, grad_o_out = collect(
        grad_attn_w, (q_cols, kv_cols, kv_cols, q_cols)
    )
    small = jnp.concatenate([grad_gain_one, grad_gain_two, grad_q_gain, grad_k_gain])
    small = sum_all(small.reshape(1, -1), dp_size)[0]
    norm_total = small[: 2 * model_dim].reshape(2, model_dim)
    head_sum = small[2 * model_dim :].reshape(2, head_dim)
    norm_own = lax.dynamic_slice_in_dim(norm_total, lax.axis_index(ALL) * shard, shard, 1)
    return (
        layer_out[None],
        input_grad[None],
        grad_q_out,
        grad_k_out,
        grad_v_out,
        grad_o_out.T,
        grad_g_out,
        grad_u_out,
        grad_d_out.T,
        norm_own.astype(BF),
        head_sum.astype(BF),
    )


def solution(mesh):
    def step(*arrays):
        return on_device(mesh.shape["dp"], *arrays)

    in_specs = (
        P("dp", "ctx", None),
        P("dp", "ctx"),
        P(("dp", "ctx"), None),
        P(("dp", "ctx"), None),
        P(("dp", "ctx"), None),
        P(None, ("dp", "ctx")),
        P(("dp", "ctx"), None),
        P(("dp", "ctx"), None),
        P(None, ("dp", "ctx")),
        P(None, ("dp", "ctx")),
        P(),
        P("dp", "ctx", None),
    )
    out_specs = (
        P("dp", "ctx", None),
        P("dp", "ctx", None),
        P(("dp", "ctx"), None),
        P(("dp", "ctx"), None),
        P(("dp", "ctx"), None),
        P(None, ("dp", "ctx")),
        P(("dp", "ctx"), None),
        P(("dp", "ctx"), None),
        P(None, ("dp", "ctx")),
        P(None, ("dp", "ctx")),
        P(),
    )
    return jax.shard_map(step, mesh=mesh, in_specs=in_specs, out_specs=out_specs, check_vma=False)
```

time: 1290 us -> 540 us (0.42)
  waiting for transfers between devices: 938 us -> 244 us
  starting transfers between devices: 1.5 us -> 66.8 us
  matrix products: 141 us -> 85.8 us
  blocking collectives: 89.4 us -> 41.8 us
  other arithmetic: 81.5 us -> 47.9 us
  local copies, waits for them, and re-layouts: 16.4 us -> 42.3 us
    reduce_scatter x4 -> x0, waiting for transfers between devices: 536 us -> none  [the longest x2 512 us: on_device(): lax.psum_scatter(jnp.concatenate([first_part, second_part], 1), ('dp', 'c...]
    all_gather x9 -> x0, waiting for transfers between devices: 398 us -> none  [the longest x1 80.5 us: on_device(): lax.all_gather(w_up, ('dp', 'ctx'), axis=0, tiled=True)]
    ppermute x0 -> x112, waiting for transfers between devices: none -> 244 us  [the longest x24 123 us: ring(): return lax.ppermute(value, 'dp', [(i, (i + 2) % size) for i in range(size)])]
    ppermute x0 -> x112, starting transfers between devices: none -> 66.8 us  [the longest x88 51.6 us: flip(): return lax.ppermute(value, axis, [(i, i ^ bits) for i in range(size)])]
    dot_general x24 -> x23, matrix products: 141 us -> 85.8 us  [the longest x7 20.4 us: dot(): lax.dot_general(a, b, (((1,), (0,)), ((), ())), preferred_element_type=F32)]
    concatenate x3 -> x5, other arithmetic: 44.7 us -> 2.84 us  [the longest x3 1.88 us: spread(): sent.append(jnp.concatenate(cut, 1))]
    psum x1 -> x0, blocking collectives: 40.9 us -> none  [on_device(): lax.psum((jnp.stack([grad_gain_one, grad_gain_two]), jnp.stack([grad_q_ga...]
    convert_element_type x6 -> x29, other arithmetic: 6.07 us -> 24.8 us  [the longest x1 8.28 us: on_device(): grad_scores = (probs * (grad_probs - inner_row)).astype(BF)]
  transfers between devices with their start and end apart: 13 -> 112, of which waited for: 12 -> 50; matrix products, arithmetic and copies ran while one was open for 14% -> 28% of each run, Pallas kernels for 0% -> 0%
where the time goes in v1:
time: 540 us; the launch traced here: 532 us
  waiting for transfers between devices  244 us (45%)
  matrix products  85.8 us (16%)
  starting transfers between devices  66.8 us (12%)
  other arithmetic  47.9 us (9%)
  local copies, waits for them, and re-layouts  42.3 us (8%)
  blocking collectives  41.8 us (8%)
    ppermute x24, waiting for transfers between devices, ring(): return lax.ppermute(value, 'dp', [(i, (i + 2) % size) for i in range(size)])  123 us
    ppermute x88, waiting for transfers between devices, flip(): return lax.ppermute(value, axis, [(i, i ^ bits) for i in range(size)])  121 us
    ppermute x88, starting transfers between devices, flip(): return lax.ppermute(value, axis, [(i, i ^ bits) for i in range(size)])  51.6 us
    all_gather x1, blocking collectives, on_device(): gains_full = lax.all_gather(norm_gains, ALL, axis=1, tiled=True).astype(F32)  41.8 us
    dot_general x7, matrix products, dot(): lax.dot_general(a, b, (((1,), (0,)), ((), ())), preferred_element_type=F32)  20.4 us
    dynamic_update_slice x68, local copies, waits for them, and re-layouts, place(): out = lax.dynamic_update_slice_in_dim(out, part, at * size, axis)  17.8 us
    dot_general x5, matrix products, dot_nt(): lax.dot_general(a, b, (((1,), (1,)), ((), ())), preferred_element_type=F32)  15.9 us
    ppermute x24, starting transfers between devices, ring(): return lax.ppermute(value, 'dp', [(i, (i + 2) % size) for i in range(size)])  15.2 us
  transfers between devices with their start and end apart: 112, of which 50 were waited for; matrix products, arithmetic and copies ran while one was open for 28% of the time, Pallas kernels for 0%

profile of v1, /device:TPU:0, one launch (start us, length us, event | category | flops | bytes accessed | tf_op | source)
XLA Modules:
  0.0 532.0 jit_solution(6411378108556584978)
XLA Ops:
  10.2 41.8 %all-gather = bf16[32,32,2]{1,2,0:T(2,128)(2,1)S(1)} all-gather(bf16[1,32,2]{1,2,0:T(2,128)(2,1)} %bitcast.173), channel_id=1, replica_groups=mesh['dp'=8,'ctx'=4] {'dp','ctx'}, dimensions={0}, use_global_device_ids=true | all-gather | bytes 4224 | tf_op jit(solution)/shard_map/all_gather | solution.py:178
  96.7 8.2 %collective-permute-done.36 = bf16[128,1152]{1,0:T(8,128)(2,1)S(1)} collective-permute-done((bf16[128,1152]{1,0:T(8,128)(2,1)S(1)}, bf16[128,1152]{1,0:T(8,128)(2,1)S(1)}, u32[]{:S(2)}, u32[]{:S(2)}) %collective-permute-start.36) | collective-permute-done | bytes 294944 | tf_op jit(solution)/shard_map/ppermute | solution.py:52
  106.3 7.9 %collective-permute-done.46 = bf16[128,1152]{1,0:T(8,128)(2,1)S(1)} collective-permute-done((bf16[128,1152]{1,0:T(8,128)(2,1)S(1)}, bf16[128,1152]{1,0:T(8,128)(2,1)S(1)}, u32[]{:S(2)}, u32[]{:S(2)}) %collective-permute-start.46) | collective-permute-done | bytes 294944 | tf_op jit(solution)/shard_map/ppermute | solution.py:52
  133.3 10.3 %collective-permute-done.38 = bf16[128,1152]{1,0:T(8,128)(2,1)} collective-permute-done((bf16[128,1152]{1,0:T(8,128)(2,1)S(1)}, bf16[128,1152]{1,0:T(8,128)(2,1)}, u32[]{:S(2)}, u32[]{:S(2)}) %collective-permute-start.38) | collective-permute-done | bytes 294944 | tf_op jit(solution)/shard_map/ppermute | solution.py:52
  179.5 7.5 %fusion.97 = (f32[2,2,1024]{2,1,0:T(2,128)S(1)}, f32[2,2,1024,1024]{2,3,1,0:T(8,128)}) fusion(bf16[1024,2,64,1]{0,2,3,1:T(8,128)(2,1)S(1)} %fusion.47, bf16[1024,2,2,64]{0,3,2,1:T(8,128)(2,1)S(1)} %fusion.34, pred[1024,1024]{0,1:T(8,128)(4,1)S(1)} %copy-done.26), kind=kOutput, calls=%fused_computation.347 | convolution fusion | flops 549449728 | bytes 18628608 | tf_op jit(solution)/shard_map/tkgd,skd->kgts/dot_general | solution.py:212
  186.9 8.0 %fusion.3 = f32[2,2,1024]{2,1,0:T(2,128)S(1)} fusion(f32[2,2,1024,1024]{2,3,1,0:T(8,128)} %get-tuple-element.138, f32[2,2,1024]{2,1,0:T(2,128)S(1)} %get-tuple-element.137), kind=kLoop, calls=%fused_computation.9 | loop fusion | flops 8384512 | bytes 16809984 | tf_op jit(solution)/shard_map/reduce_sum | solution.py:219
  194.9 7.5 %fusion.18 = bf16[2,64,2,1024]{3,1,2,0:T(8,128)(2,1)S(1)} fusion(bf16[1024,2,64,1]{0,2,3,1:T(8,128)(2,1)S(1)} %bitcast.152, f32[2,2,1024,1024]{2,3,1,0:T(8,128)} %get-tuple-element.138, f32[2,2,1024]{2,1,0:T(2,128)S(1)} %fusion.3, f32[2,2,1024]{2,1,0:T(2,128)S(1)} %get-tuple-element.137), kind=kOutput, calls=%fused_computation.68 | convolution fusion | flops 549715968 | bytes 17596416 | tf_op jit(solution)/shard_map/kgts,skd->tkgd/dot_general | solution.py:222
  206.4 13.0 %collective-permute-start.50 = (bf16[128,1152]{1,0:T(8,128)(2,1)}, bf16[128,1152]{1,0:T(8,128)(2,1)S(1)}, u32[]{:S(2)}, u32[]{:S(2)}) collective-permute-start(bf16[128,1152]{1,0:T(8,128)(2,1)} %collective-permute-done.48), channel_id=1, source_target_pairs={{0,8},{4,12},{8,16},{12,20},{16,24},{20,28},{24,0},{28,4},{1,9},{5... | collective-permute-start | bytes 884744 | tf_op jit(solution)/shard_map/ppermute | solution.py:52
  221.2 9.1 %collective-permute-done.50 = bf16[128,1152]{1,0:T(8,128)(2,1)S(1)} collective-permute-done((bf16[128,1152]{1,0:T(8,128)(2,1)}, bf16[128,1152]{1,0:T(8,128)(2,1)S(1)}, u32[]{:S(2)}, u32[]{:S(2)}) %collective-permute-start.50) | collective-permute-done | bytes 294944 | tf_op jit(solution)/shard_map/ppermute | solution.py:52
  236.5 15.1 %collective-permute-done.41 = bf16[128,1152]{1,0:T(8,128)(2,1)S(1)} collective-permute-done((bf16[128,1152]{1,0:T(8,128)(2,1)}, bf16[128,1152]{1,0:T(8,128)(2,1)S(1)}, u32[]{:S(2)}, u32[]{:S(2)}) %collective-permute-start.41) | collective-permute-done | bytes 294944 | tf_op jit(solution)/shard_map/ppermute | solution.py:20
  252.9 11.4 %collective-permute-done.20 = bf16[256,1024]{1,0:T(8,128)(2,1)S(1)} collective-permute-done((bf16[256,1024]{1,0:T(8,128)(2,1)S(1)}, bf16[256,1024]{1,0:T(8,128)(2,1)S(1)}, u32[]{:S(2)}, u32[]{:S(2)}) %collective-permute-start.20) | collective-permute-done | bytes 524320 | tf_op jit(solution)/shard_map/ppermute | solution.py:20
  273.3 8.2 %fusion.13 = (bf16[1024,1152]{1,0:T(8,128)(2,1)}, bf16[1024,1152]{1,0:T(8,128)(2,1)}, bf16[1024,1152]{1,0:T(8,128)(2,1)S(1)}) fusion(f32[1024,1152]{1,0:T(8,128)S(1)} %fusion.46, f32[1024,1152]{1,0:T(8,128)S(1)} %fusion.77, bf16[1024,1152]{1,0:T(8,128)(2,1)S(1)} %constant_dynamic-update-slice_fusion.47, bf16[256,1024]{1,0:T(8,128)(2,1)S(1)} %collective-permute-done.21, ...), kind=kOutput, calls=%fused_computation.21 | convolution fusion | flops 2443182080 | bytes 20971520 | tf_op jit(solution)/shard_map/dot_general | solution.py:100
  310.4 7.9 %collective-permute-done.90 = bf16[128,1152]{1,0:T(8,128)(2,1)S(1)} collective-permute-done((bf16[128,1152]{1,0:T(8,128)(2,1)S(1)}, bf16[128,1152]{1,0:T(8,128)(2,1)S(1)}, u32[]{:S(2)}, u32[]{:S(2)}) %collective-permute-start.90) | collective-permute-done | bytes 294944 | tf_op jit(solution)/shard_map/ppermute | solution.py:20
  318.9 8.0 %collective-permute-done.80 = bf16[128,1152]{1,0:T(8,128)(2,1)S(1)} collective-permute-done((bf16[128,1152]{1,0:T(8,128)(2,1)S(1)}, bf16[128,1152]{1,0:T(8,128)(2,1)S(1)}, u32[]{:S(2)}, u32[]{:S(2)}) %collective-permute-start.80) | collective-permute-done | bytes 294944 | tf_op jit(solution)/shard_map/ppermute | solution.py:20
  329.5 8.7 %collective-permute-done.101 = bf16[128,1152]{1,0:T(8,128)(2,1)S(1)} collective-permute-done((bf16[128,1152]{1,0:T(8,128)(2,1)S(1)}, bf16[128,1152]{1,0:T(8,128)(2,1)S(1)}, u32[]{:S(2)}, u32[]{:S(2)}) %collective-permute-start.101) | collective-permute-done | bytes 294944 | tf_op jit(solution)/shard_map/ppermute | solution.py:52
  338.8 9.9 %collective-permute-done.91 = bf16[128,1152]{1,0:T(8,128)(2,1)S(1)} collective-permute-done((bf16[128,1152]{1,0:T(8,128)(2,1)S(1)}, bf16[128,1152]{1,0:T(8,128)(2,1)S(1)}, u32[]{:S(2)}, u32[]{:S(2)}) %collective-permute-start.91) | collective-permute-done | bytes 294944 | tf_op jit(solution)/shard_map/ppermute | solution.py:52
  349.2 9.1 %collective-permute-done.81 = bf16[128,1152]{1,0:T(8,128)(2,1)S(1)} collective-permute-done((bf16[128,1152]{1,0:T(8,128)(2,1)S(1)}, bf16[128,1152]{1,0:T(8,128)(2,1)S(1)}, u32[]{:S(2)}, u32[]{:S(2)}) %collective-permute-start.81) | collective-permute-done | bytes 294944 | tf_op jit(solution)/shard_map/ppermute | solution.py:52
  358.8 8.1 %collective-permute-done.102 = bf16[128,1152]{1,0:T(8,128)(2,1)S(1)} collective-permute-done((bf16[128,1152]{1,0:T(8,128)(2,1)S(1)}, bf16[128,1152]{1,0:T(8,128)(2,1)S(1)}, u32[]{:S(2)}, u32[]{:S(2)}) %collective-permute-start.102) | collective-permute-done | bytes 294944 | tf_op jit(solution)/shard_map/ppermute | solution.py:52
  367.4 8.0 %collective-permute-done.92 = bf16[128,1152]{1,0:T(8,128)(2,1)S(1)} collective-permute-done((bf16[128,1152]{1,0:T(8,128)(2,1)S(1)}, bf16[128,1152]{1,0:T(8,128)(2,1)S(1)}, u32[]{:S(2)}, u32[]{:S(2)}) %collective-permute-start.92) | collective-permute-done | bytes 294944 | tf_op jit(solution)/shard_map/ppermute | solution.py:52
  375.9 8.0 %collective-permute-done.82 = bf16[128,1152]{1,0:T(8,128)(2,1)S(1)} collective-permute-done((bf16[128,1152]{1,0:T(8,128)(2,1)S(1)}, bf16[128,1152]{1,0:T(8,128)(2,1)S(1)}, u32[]{:S(2)}, u32[]{:S(2)}) %collective-permute-start.82) | collective-permute-done | bytes 294944 | tf_op jit(solution)/shard_map/ppermute | solution.py:52
  428.2 8.5 %fusion = (f32[2,2,1024]{2,1,0:T(2,128)S(1)}, f32[2,1024,1024,2]{2,1,3,0:T(8,128)}) fusion(f32[2,2,1024,1024]{2,3,1,0:T(8,128)S(1)} %bitcast.139, f32[2,2,1024]{2,1,0:T(2,128)S(1)} %log_add_fusion, bf16[1024,2,64,1]{0,2,3,1:T(8,128)(2,1)} %bitcast.153, bf16[1024,2,2,64]{0,3,2,1:T(8,128)(2,1)S(1)} %bitcast.149), kind=kOutput, calls=%fused_computation.2 | convolution fusion | flops 549449728 | bytes 34373632 | tf_op jit(solution)/shard_map/tkgd,skd->kgts/dot_general | solution.py:266
  436.7 8.3 %fusion.2 = bf16[2,2,1024,1024]{2,3,1,0:T(8,128)(2,1)S(1)} fusion(f32[2,1024,1024,2]{2,1,3,0:T(8,128)} %get-tuple-element.140, f32[2,2,1024,1024]{2,3,1,0:T(8,128)S(1)} %bitcast.139, f32[2,2,1024]{2,1,0:T(2,128)S(1)} %get-tuple-element.139, f32[2,2,1024]{2,1,0:T(2,128)S(1)} %log_add_fusion), kind=kLoop, calls=%fused_computation.4 | loop fusion | flops 16777216 | bytes 41975808 | tf_op jit(solution)/shard_map/convert_element_type | solution.py:273
  492.9 7.6 %collective-permute-done.72 = bf16[128,768]{0,1:T(8,128)(2,1)} collective-permute-done((bf16[128,768]{0,1:T(8,128)(2,1)}, bf16[128,768]{0,1:T(8,128)(2,1)}, u32[]{:S(2)}, u32[]{:S(2)}) %collective-permute-start.72) | collective-permute-done | bytes 196640 | tf_op jit(solution)/shard_map/ppermute | solution.py:52
  512.8 8.9 %collective-permute-done.76 = bf16[32,768]{0,1:T(8,128)(2,1)S(1)} collective-permute-done((bf16[32,768]{0,1:T(8,128)(2,1)S(1)}, bf16[32,768]{0,1:T(8,128)(2,1)S(1)}, u32[]{:S(2)}, u32[]{:S(2)}) %collective-permute-start.76) | collective-permute-done | bytes 49184 | tf_op jit(solution)/shard_map/ppermute | solution.py:20
  (552 shorter events, 280.0 us)
Async XLA Ops:
  0.7 56.2 %collective-permute-start.13 = (s32[1,256]{1,0:T(1,128)}, s32[1,256]{1,0:T(1,128)S(1)}, u32[]{:S(2)}, u32[]{:S(2)}) collective-permute-start(s32[1,256]{1,0:T(1,128)} %param.13), channel_id=1, source_target_pairs={{0,1},{1,0},{2,3},{3,2},{4,5},{5,4},{6,7},{7,6},{8,9},{9,8},{10,11... | collective-permute-start | bytes 3080 | tf_op jit(solution)/shard_map/ppermute | solution.py:20
  1.2 55.3 %collective-permute-start.14 = (s32[1,256]{1,0:T(1,128)}, s32[1,256]{1,0:T(1,128)S(1)}, u32[]{:S(2)}, u32[]{:S(2)}) collective-permute-start(s32[1,256]{1,0:T(1,128)} %param.13), channel_id=1, source_target_pairs={{0,2},{1,3},{2,0},{3,1},{4,6},{5,7},{6,4},{7,5},{8,10},{9,11},{10,... | collective-permute-start | bytes 3080 | tf_op jit(solution)/shard_map/ppermute | solution.py:20
  3.7 141.6 %collective-permute-start.1 = (bf16[256,1024]{1,0:T(8,128)(2,1)}, bf16[256,1024]{1,0:T(8,128)(2,1)S(1)}, u32[]{:S(2)}, u32[]{:S(2)}) collective-permute-start(bf16[256,1024]{1,0:T(8,128)(2,1)} %bitcast.143), channel_id=1, source_target_pairs={{0,2},{1,3},{2,0},{3,1},{4,6},{5,7},{6,4},{7,5},{8,10},{9,11},{10,... | collective-permute-start | bytes 1572872 | tf_op jit(solution)/shard_map/ppermute | solution.py:20
  3.8 164.2 %collective-permute-start = (bf16[256,1024]{1,0:T(8,128)(2,1)}, bf16[256,1024]{1,0:T(8,128)(2,1)S(1)}, u32[]{:S(2)}, u32[]{:S(2)}) collective-permute-start(bf16[256,1024]{1,0:T(8,128)(2,1)} %bitcast.144), channel_id=1, source_target_pairs={{0,1},{1,0},{2,3},{3,2},{4,5},{5,4},{6,7},{7,6},{8,9},{9,8},{10,11... | collective-permute-start | bytes 1572872 | tf_op jit(solution)/shard_map/ppermute | solution.py:20
  7.6 56.2 %collective-permute-start.4 = (bf16[32,768]{1,0:T(8,128)(2,1)}, bf16[32,768]{1,0:T(8,128)(2,1)S(1)}, u32[]{:S(2)}, u32[]{:S(2)}) collective-permute-start(bf16[32,768]{1,0:T(8,128)(2,1)} %pad_maximum_fusion.13), channel_id=1, source_target_pairs={{0,2},{1,3},{2,0},{3,1},{4,6},{5,7},{6,4},{7,5},{8,10},{9,11},{10,... | collective-permute-start | bytes 147464 | tf_op jit(solution)/shard_map/ppermute | solution.py:20
  91.0 23.3 %collective-permute-start.26 = (bf16[128,1152]{1,0:T(8,128)(2,1)S(1)}, bf16[128,1152]{1,0:T(8,128)(2,1)S(1)}, u32[]{:S(2)}, u32[]{:S(2)}) collective-permute-start(bf16[128,1152]{1,0:T(8,128)(2,1)S(1)} %constant_dynamic-update-slice_fusion.55), channel_id=1, source_target_pairs={{0,8},{4,12},{8,16},{12,20},{16,24},{20,28},{24,0},{28,4},{1,9},{5... | collective-permute-start | bytes 884744 | tf_op jit(solution)/shard_map/ppermute | solution.py:52
  130.3 26.8 %collective-permute-start.56 = (bf16[256,1024]{1,0:T(8,128)(2,1)}, bf16[256,1024]{1,0:T(8,128)(2,1)}, u32[]{:S(2)}, u32[]{:S(2)}) collective-permute-start(bf16[256,1024]{1,0:T(8,128)(2,1)} %bitcast.31), channel_id=1, source_target_pairs={{0,2},{1,3},{2,0},{3,1},{4,6},{5,7},{6,4},{7,5},{8,10},{9,11},{10,... | collective-permute-start | bytes 1572872 | tf_op jit(solution)/shard_map/ppermute | solution.py:20
  157.1 107.2 %collective-permute-start.55 = (bf16[256,1024]{1,0:T(8,128)(2,1)}, bf16[256,1024]{1,0:T(8,128)(2,1)}, u32[]{:S(2)}, u32[]{:S(2)}) collective-permute-start(bf16[256,1024]{1,0:T(8,128)(2,1)} %bitcast.31), channel_id=1, source_target_pairs={{0,1},{1,0},{2,3},{3,2},{4,5},{5,4},{6,7},{7,6},{8,9},{9,8},{10,11... | collective-permute-start | bytes 1572872 | tf_op jit(solution)/shard_map/ppermute | solution.py:20
  161.0 103.3 %collective-permute-start.57 = (bf16[256,1024]{1,0:T(8,128)(2,1)}, bf16[256,1024]{1,0:T(8,128)(2,1)}, u32[]{:S(2)}, u32[]{:S(2)}) collective-permute-start(bf16[256,1024]{1,0:T(8,128)(2,1)} %collective-permute-done.56), channel_id=1, source_target_pairs={{0,1},{1,0},{2,3},{3,2},{4,5},{5,4},{6,7},{7,6},{8,9},{9,8},{10,11... | collective-permute-start | bytes 1572872 | tf_op jit(solution)/shard_map/ppermute | solution.py:20
  167.0 39.4 %collective-permute-start.29 = (bf16[128,1152]{1,0:T(8,128)(2,1)}, bf16[128,1152]{1,0:T(8,128)(2,1)}, u32[]{:S(2)}, u32[]{:S(2)}) collective-permute-start(bf16[128,1152]{1,0:T(8,128)(2,1)} %collective-permute-done.28), channel_id=1, source_target_pairs={{0,4},{4,0},{8,12},{12,8},{16,20},{20,16},{24,28},{28,24},{1,5},{5... | collective-permute-start | bytes 884744 | tf_op jit(solution)/shard_map/ppermute | solution.py:20
  168.0 37.4 %collective-permute-start.49 = (bf16[128,1152]{1,0:T(8,128)(2,1)}, bf16[128,1152]{1,0:T(8,128)(2,1)}, u32[]{:S(2)}, u32[]{:S(2)}) collective-permute-start(bf16[128,1152]{1,0:T(8,128)(2,1)} %collective-permute-done.48), channel_id=1, source_target_pairs={{0,4},{4,0},{8,12},{12,8},{16,20},{20,16},{24,28},{28,24},{1,5},{5... | collective-permute-start | bytes 884744 | tf_op jit(solution)/shard_map/ppermute | solution.py:20
  169.8 33.6 %collective-permute-start.40 = (bf16[128,1152]{1,0:T(8,128)(2,1)}, bf16[128,1152]{1,0:T(8,128)(2,1)}, u32[]{:S(2)}, u32[]{:S(2)}) collective-permute-start(bf16[128,1152]{1,0:T(8,128)(2,1)} %collective-permute-done.38), channel_id=1, source_target_pairs={{0,8},{4,12},{8,16},{12,20},{16,24},{20,28},{24,0},{28,4},{1,9},{5... | collective-permute-start | bytes 884744 | tf_op jit(solution)/shard_map/ppermute | solution.py:52
  206.4 23.9 %collective-permute-start.50 = (bf16[128,1152]{1,0:T(8,128)(2,1)}, bf16[128,1152]{1,0:T(8,128)(2,1)S(1)}, u32[]{:S(2)}, u32[]{:S(2)}) collective-permute-start(bf16[128,1152]{1,0:T(8,128)(2,1)} %collective-permute-done.48), channel_id=1, source_target_pairs={{0,8},{4,12},{8,16},{12,20},{16,24},{20,28},{24,0},{28,4},{1,9},{5... | collective-permute-start | bytes 884744 | tf_op jit(solution)/shard_map/ppermute | solution.py:52
  230.3 22.4 %collective-permute-start.31 = (bf16[128,1152]{1,0:T(8,128)(2,1)S(1)}, bf16[128,1152]{1,0:T(8,128)(2,1)S(1)}, u32[]{:S(2)}, u32[]{:S(2)}) collective-permute-start(bf16[128,1152]{1,0:T(8,128)(2,1)S(1)} %collective-permute-done.30), channel_id=1, source_target_pairs={{0,4},{4,0},{8,12},{12,8},{16,20},{20,16},{24,28},{28,24},{1,5},{5... | collective-permute-start | bytes 884744 | tf_op jit(solution)/shard_map/ppermute | solution.py:20
  230.7 22.0 %collective-permute-start.51 = (bf16[128,1152]{1,0:T(8,128)(2,1)S(1)}, bf16[128,1152]{1,0:T(8,128)(2,1)S(1)}, u32[]{:S(2)}, u32[]{:S(2)}) collective-permute-start(bf16[128,1152]{1,0:T(8,128)(2,1)S(1)} %collective-permute-done.50), channel_id=1, source_target_pairs={{0,4},{4,0},{8,12},{12,8},{16,20},{20,16},{24,28},{28,24},{1,5},{5... | collective-permute-start | bytes 884744 | tf_op jit(solution)/shard_map/ppermute | solution.py:20
  284.7 102.2 %collective-permute-start.52 = (bf16[256,1024]{1,0:T(8,128)(2,1)S(1)}, bf16[256,1024]{1,0:T(8,128)(2,1)S(1)}, u32[]{:S(2)}, u32[]{:S(2)}) collective-permute-start(bf16[256,1024]{1,0:T(8,128)(2,1)S(1)} %get-tuple-element.46), channel_id=1, source_target_pairs={{0,1},{1,0},{2,3},{3,2},{4,5},{5,4},{6,7},{7,6},{8,9},{9,8},{10,11... | collective-permute-start | bytes 1572872 | tf_op jit(solution)/shard_map/ppermute | solution.py:20
  285.3 41.7 %collective-permute-start.53 = (bf16[256,1024]{1,0:T(8,128)(2,1)S(1)}, bf16[256,1024]{1,0:T(8,128)(2,1)S(1)}, u32[]{:S(2)}, u32[]{:S(2)}) collective-permute-start(bf16[256,1024]{1,0:T(8,128)(2,1)S(1)} %get-tuple-element.47), channel_id=1, source_target_pairs={{0,1},{1,0},{2,3},{3,2},{4,5},{5,4},{6,7},{7,6},{8,9},{9,8},{10,11... | collective-permute-start | bytes 1572872 | tf_op jit(solution)/shard_map/ppermute | solution.py:20
  290.3 38.9 %collective-permute-start.99 = (bf16[128,1152]{1,0:T(8,128)(2,1)S(1)}, bf16[128,1152]{1,0:T(8,128)(2,1)S(1)}, u32[]{:S(2)}, u32[]{:S(2)}) collective-permute-start(bf16[128,1152]{1,0:T(8,128)(2,1)S(1)} %get-tuple-element.32), channel_id=1, source_target_pairs={{0,4},{4,0},{8,12},{12,8},{16,20},{20,16},{24,28},{28,24},{1,5},{5... | collective-permute-start | bytes 884744 | tf_op jit(solution)/shard_map/ppermute | solution.py:20
  292.1 66.3 %collective-permute-start.98 = (bf16[128,1152]{1,0:T(8,128)(2,1)S(1)}, bf16[128,1152]{1,0:T(8,128)(2,1)S(1)}, u32[]{:S(2)}, u32[]{:S(2)}) collective-permute-start(bf16[128,1152]{1,0:T(8,128)(2,1)S(1)} %get-tuple-element.33), channel_id=1, source_target_pairs={{0,4},{4,0},{8,12},{12,8},{16,20},{20,16},{24,28},{28,24},{1,5},{5... | collective-permute-start | bytes 884744 | tf_op jit(solution)/shard_map/ppermute | solution.py:20
  328.8 55.5 %collective-permute-start.58 = (bf16[256,1024]{1,0:T(8,128)(2,1)S(1)}, bf16[256,1024]{1,0:T(8,128)(2,1)S(1)}, u32[]{:S(2)}, u32[]{:S(2)}) collective-permute-start(bf16[256,1024]{1,0:T(8,128)(2,1)S(1)} %get-tuple-element.44), channel_id=1, source_target_pairs={{0,1},{1,0},{2,3},{3,2},{4,5},{5,4},{6,7},{7,6},{8,9},{9,8},{10,11... | collective-permute-start | bytes 1572872 | tf_op jit(solution)/shard_map/ppermute | solution.py:20
  415.0 58.1 %collective-permute-start.86 = (bf16[32,1152]{1,0:T(8,128)(2,1)S(1)}, bf16[32,1152]{1,0:T(8,128)(2,1)S(1)}, u32[]{:S(2)}, u32[]{:S(2)}) collective-permute-start(bf16[32,1152]{1,0:T(8,128)(2,1)S(1)} %get-tuple-element.71), channel_id=1, source_target_pairs={{0,3},{1,2},{2,1},{3,0},{4,7},{5,6},{6,5},{7,4},{8,11},{9,10},{10,... | collective-permute-start | bytes 221192 | tf_op jit(solution)/shard_map/ppermute | solution.py:20
  473.7 31.1 %collective-permute-start.67 = (bf16[128,768]{0,1:T(8,128)(2,1)}, bf16[128,768]{0,1:T(8,128)(2,1)S(1)}, u32[]{:S(2)}, u32[]{:S(2)}) collective-permute-start(bf16[128,768]{0,1:T(8,128)(2,1)} %get-tuple-element.50), channel_id=1, source_target_pairs={{0,4},{4,0},{8,12},{12,8},{16,20},{20,16},{24,28},{28,24},{1,5},{5... | collective-permute-start | bytes 589832 | tf_op jit(solution)/shard_map/ppermute | solution.py:20
  482.7 44.6 %collective-permute-start.64 = (bf16[256,1024]{1,0:T(8,128)(2,1)}, bf16[256,1024]{1,0:T(8,128)(2,1)}, u32[]{:S(2)}, u32[]{:S(2)}) collective-permute-start(bf16[256,1024]{1,0:T(8,128)(2,1)} %get-tuple-element.42), channel_id=1, source_target_pairs={{0,1},{1,0},{2,3},{3,2},{4,5},{5,4},{6,7},{7,6},{8,9},{9,8},{10,11... | collective-permute-start | bytes 1572872 | tf_op jit(solution)/shard_map/ppermute | solution.py:20
  503.7 23.6 %collective-permute-start.66 = (bf16[256,1024]{1,0:T(8,128)(2,1)}, bf16[256,1024]{1,0:T(8,128)(2,1)}, u32[]{:S(2)}, u32[]{:S(2)}) collective-permute-start(bf16[256,1024]{1,0:T(8,128)(2,1)} %add_convert_fusion.1), channel_id=1, source_target_pairs={{0,2},{1,3},{2,0},{3,1},{4,6},{5,7},{6,4},{7,5},{8,10},{9,11},{10,... | collective-permute-start | bytes 1572872 | tf_op jit(solution)/shard_map/ppermute | solution.py:20
  (146 other events, 1807.2 us)
